TPU v7x, 256 devices: a whole 4x4x8 slice. The times are simulated.
256 devices in a mesh: ctx: 64 (over x_hi, z, y), head: 4 (over x_lo, core).
Axes of the slice: x: 4 (x_hi: 2, x_lo: 2; x = x_hi * 2 + x_lo), y: 4, z: 8, core: 2. Of those that a mesh axis runs over, the one named last changes fastest.
Arguments:
- queries: bfloat16 [8192, 4096], P('ctx', 'head'), may hold values from -81 to 81
- key_states: bfloat16 [8192, 1024], P('ctx', 'head'), may hold values from -7 to 7
- value_states: bfloat16 [8192, 1024], P('ctx', 'head'), may hold values from -6 to 6
- out_weight: bfloat16 [4096, 4096], P('head'), may hold values from -0.09375 to 0.09375
- head_role: int32 [8], replicated, may hold values from 0 to 1, as said below
- sink_len: int32 [8], replicated, may hold values from 32 to 128, as said below
- window_len: int32 [8], replicated, may hold values from 256 to 1024, as said below
Outputs:
- mixed: bfloat16 [8192, 4096], P(('ctx', 'head'))
Inputs may be any that keep to these rules, and one draw needn't show every extreme that they name: `head_role`: exactly 4 heads are retrieval heads. `sink_len`: some head has exactly 128. `window_len`: some head has exactly 1024.
All inputs are finite; a program needn't handle non-finite values.
Results may differ from a plain program's by a relative error of at most 0.012.
Values may be sent and summed in bfloat16 or wider, within the bound.
A program may use at most 128 MiB of HBM per device.

v0:
```python
import jax
import jax.numpy as jnp
from jax import lax
from jax.sharding import PartitionSpec as P

HD = 128
GROUP = 4
NEGATIVE = -1e30


def online_update(running, query_heads, key_part, value_part, allowed):
    row_peak, row_total, weighted = running
    scores = jnp.einsum(
        "thgd,jhd->thgj", query_heads, key_part, preferred_element_type=jnp.float32
    ) * HD ** (-0.5)
    visible = allowed[:, :, None, :]
    block_peak = jnp.max(jnp.where(visible, scores, NEGATIVE), axis=-1)
    new_peak = jnp.maximum(row_peak, block_peak)
    weights = jnp.where(visible, jnp.exp(scores - new_peak[..., None]), 0.0)
    row_total = jnp.sum(weights, axis=-1)
    weighted = jnp.einsum(
        "thgj,jhd->thgd",
        weights.astype(jnp.bfloat16),
        value_part,
        preferred_element_type=jnp.float32,
    )
    return (new_peak, row_total, weighted)


def empty_state(row_count, head_count):
    return (
        jnp.full((row_count, head_count, GROUP), NEGATIVE, jnp.float32),
        jnp.zeros((row_count, head_count, GROUP), jnp.float32),
        jnp.zeros((row_count, head_count, GROUP, HD), jnp.float32),
    )


def finish(running, row_count):
    row_peak, row_total, weighted = running
    return (weighted / row_total[..., None]).astype(jnp.bfloat16).reshape(row_count, -1)


def per_device(queries, key_states, value_states, out_weight, head_role, sink_len, window_len):
    row_count = queries.shape[0]
    local_heads = key_states.shape[1] // HD
    row_base = lax.axis_index("ctx") * row_count
    query_pos = row_base + jnp.arange(row_count, dtype=jnp.int32)
    my_group = lax.axis_index("head")
    first_head = my_group * local_heads
    last_row = row_base + row_count - 1
    roles_here = lax.dynamic_slice_in_dim(head_role, first_head, local_heads)
    sinks_here = lax.dynamic_slice_in_dim(sink_len, first_head, local_heads)
    windows_here = lax.dynamic_slice_in_dim(window_len, first_head, local_heads)
    query_heads = queries.reshape(row_count, local_heads, GROUP, HD)
    key_part = lax.all_gather(key_states, "ctx", axis=0, tiled=True).reshape(-1, local_heads, HD)
    value_part = lax.all_gather(value_states, "ctx", axis=0, tiled=True).reshape(
        -1, local_heads, HD
    )
    key_pos = jnp.arange(key_part.shape[0], dtype=jnp.int32)

    def update(state):
        later = query_pos[:, None, None]
        earlier = key_pos[None, None, :]
        allowed = (earlier <= later) & (
            (roles_here[None, :, None] == 1)
            | (earlier < sinks_here[None, :, None])
            | (later - earlier < windows_here[None, :, None])
        )
        return online_update(state, query_heads, key_part, value_part, allowed)

    def unchanged(state):
        return state

    running = lax.cond(
        jnp.int32(0) <= last_row, update, unchanged, empty_state(row_count, local_heads)
    )
    attended = finish(running, row_count)
    mixed = lax.psum_scatter(
        jnp.dot(attended, out_weight, preferred_element_type=jnp.float32).astype(jnp.bfloat16),
        "head",
        scatter_dimension=0,
        tiled=True,
    )
    return mixed


def solution(mesh):
    in_specs = (
        P("ctx", "head"),
        P("ctx", "head"),
        P("ctx", "head"),
        P("head", None),
        P(),
        P(),
        P(),
    )
    out_specs = P(("ctx", "head"), None)
    return jax.shard_map(
        per_device, mesh=mesh, in_specs=in_specs, out_specs=out_specs, check_vma=False
    )
```

profile of v0, /device:TPU:1, one launch (start us, length us, event | category | flops | bytes accessed | tf_op | source)
XLA Modules:
  0.0 373.8 jit_solution(10370154354749702863)
XLA Ops:
  6.5 0.7 all-gather.3.cloned.1.call-update
  7.3 0.0 all-gather.5.cloned.1.call-start
  7.3 0.7 all-gather.5.cloned.1.call-update
  8.0 0.0 reduce-scatter.2.cloned.1.call-start
  8.1 131.3 %all-gather.3.cloned.1.call-done = bf16[8192,256]{1,0:T(8,128)(2,1)} async-done(((bf16[128,256]{1,0:T(8,128)(2,1)}), bf16[8192,256]{1,0:T(8,128)(2,1)}) %all-gather.3.cloned.1.call-update) | async-done | bytes 4194320 | tf_op jit(solution)/shard_map/all_gather | solution.py:55
  139.4 128.3 %all-gather.5.cloned.1.call-done = bf16[8192,256]{1,0:T(8,128)(2,1)} async-done(((bf16[128,256]{1,0:T(8,128)(2,1)}), bf16[8192,256]{1,0:T(8,128)(2,1)}) %all-gather.5.cloned.1.call-update) | async-done | bytes 4194320 | tf_op jit(solution)/shard_map/all_gather | solution.py:56
  267.6 70.6 %conditional.1 = (f32[128,2,4]{0,2,1:T(4,128)S(1)}, f32[128,2,4,128]{0,3,2,1:T(8,128)S(1)}) conditional(s32[]{:T(128)} %convert_element_type.15, () %tuple.22, (s32[8192]{0:T(1024)S(1)}, s32[8192]{0:T(1024)S(1)}, s32[]{:T(128)}, s32[128]{0:T(128)S(1)}, s32[]{:T(128)}, /*index=5*/s32[8]{0:T(128)}, s32[8192]{0:T(1024)S(1)}, s32[8]{0:T(128)}, ...), branch_computations={%region_0.0_spmd, %region_1.4_spmd} | conditional | flops 4395662336 | bytes 148269232 | solution.py:74
  267.6 0.7 dynamic-slice_compare_fusion
  268.4 0.7 dynamic_slice.19
  269.1 0.1 compare_or_fusion
  269.2 0.7 dynamic_slice.20
  269.9 1.2 broadcast_subtract_fusion
  271.2 3.7 broadcast_compare_fusion
  274.9 2.8 or_and_fusion
  277.7 6.9 %reshape.125 = bf16[8192,2,128]{2,1,0:T(2,128)(2,1)} reshape(bf16[8192,256]{1,0:T(8,128)(2,1)} %get-tuple-element.125) | data formatting | bytes 8388608 | tf_op jit(solution)/shard_map/reshape | solution.py:55
  284.6 0.2 reshape.126
  284.8 15.7 %fusion = (f32[128,2,4]{0,2,1:T(4,128)S(1)}, f32[2,8192,128,4]{2,1,3,0:T(8,128)}) fusion(pred[128,2,8192]{0,2,1:T(8,128)(4,1)S(1)} %or_and_fusion, bf16[128,2,4,128]{3,2,1,0:T(4,128)(2,1)S(1)} %reshape.126, bf16[8192,2,128,1]{2,1,0,3:T(2,128)(2,1)} %bitcast.23), kind=kOutput, calls=%fused_computation.2 | convolution fusion | flops 2172648448 | bytes 40112128 | tf_op jit(solution)/shard_map/cond/branch_1_fun/thgd,jhd->thgj/dot_general | solution.py:13
  300.5 6.9 %reshape.127 = bf16[8192,2,128]{2,1,0:T(2,128)(2,1)} reshape(bf16[8192,256]{1,0:T(8,128)(2,1)} %get-tuple-element.127) | data formatting | bytes 8388608 | tf_op jit(solution)/shard_map/reshape | solution.py:56
  307.4 16.3 %fusion.11 = f32[128,2,4,128]{3,0,2,1:T(8,128)S(1)} fusion(bf16[8192,2,128,1]{2,1,0,3:T(2,128)(2,1)} %bitcast.24, f32[2,8192,128,4]{2,1,3,0:T(8,128)} %get-tuple-element.142, f32[128,2,4]{0,2,1:T(4,128)S(1)} %broadcast_maximum_fusion, pred[128,2,8192]{0,2,1:T(8,128)(4,1)S(1)} %or_and_fusion), kind=kOutput, calls=%fused_computation.15 | convolution fusion | flops 2181038080 | bytes 40374272 | tf_op jit(solution)/shard_map/cond/branch_1_fun/thgj,jhd->thgd/dot_general | solution.py:21
  323.7 0.2 copy.36
  323.9 14.3 %fusion.4 = f32[128,2,4]{0,2,1:T(4,128)S(1)} fusion(f32[2,8192,128,4]{2,1,3,0:T(8,128)} %get-tuple-element.142, f32[128,2,4]{0,2,1:T(4,128)S(1)} %broadcast_maximum_fusion, pred[128,2,8192]{0,2,1:T(8,128)(4,1)S(1)} %or_and_fusion), kind=kLoop, calls=%fused_computation.6 | loop fusion | flops 33553408 | bytes 35659776 | tf_op jit(solution)/shard_map/cond/branch_1_fun/reduce_sum | solution.py:20
  338.3 0.1 divide_convert_fusion
  338.3 5.6 %convolution_convert_fusion = bf16[128,4096]{1,0:T(8,128)(2,1)} fusion(bf16[128,1024]{0,1:T(8,128)(2,1)S(1)} %bitcast.25, bf16[1024,4096]{1,0:T(8,128)(2,1)} %param.12), kind=kOutput, calls=%fused_computation.23 | convolution fusion | flops 1074266112 | bytes 9699328 | tf_op jit(solution)/shard_map/dot_general | solution.py:79
  344.0 23.3 %reduce-scatter.2.cloned.1.call-done = bf16[32,4096]{1,0:T(8,128)(2,1)} async-done(((bf16[128,4096]{1,0:T(8,128)(2,1)}), bf16[32,4096]{1,0:T(8,128)(2,1)}) %reduce-scatter.2.cloned.1.call-update) | async-done | bytes 262160 | tf_op jit(solution)/shard_map/reduce_scatter | solution.py:78
  (8 shorter events, 0.0 us)
Async XLA Ops:
  6.5 132.8 %all-gather.3.cloned.1.call-start = ((), (), s32[]{:S(2)}) async-start(), calls=%async_computation.1 | async-start | bytes 4259840 | tf_op jit(solution)/shard_map/all_gather | solution.py:55
  7.3 260.4 %all-gather.5.cloned.1.call-start = ((), (), s32[]{:S(2)}) async-start(), calls=%async_computation.2 | async-start | bytes 4259840 | tf_op jit(solution)/shard_map/all_gather | solution.py:56
  8.0 359.3 %reduce-scatter.2.cloned.1.call-start = ((), (), s32[]{:S(2)}) async-start(), calls=%async_computation.3 | async-start | bytes 1310720 | tf_op jit(solution)/shard_map/reduce_scatter | solution.py:78
  271.2 13.4 %copy-start = (bf16[128,1024]{1,0:T(8,128)(2,1)S(1)}, bf16[128,1024]{1,0:T(8,128)(2,1)}, u32[]{:S(2)}) copy-start(bf16[128,1024]{1,0:T(8,128)(2,1)} %get-tuple-element.139) | copy-start | bytes 786436 | tf_op jit(solution)/shard_map/cond
Sparse Core Ops, SparseCore 0:
  10.9 128.4 all-gather.2
  142.9 124.6 all-gather.4
  344.1 23.1 reduce-scatter.1
where the time goes:
time: 374 us
  waiting for transfers between devices  284 us (76%)
  matrix products  37.7 us (10%)
  other arithmetic  23 us (6%)
  local copies, waits for them, and re-layouts  15.6 us (4%)
  between operations  13.1 us (4%)
    all_gather x1, waiting for transfers between devices, per_device(): lax.all_gather(key_states, 'ctx', axis=0, tiled=True)  131 us
    all_gather x1, waiting for transfers between devices, per_device(): lax.all_gather(value_states, 'ctx', axis=0, tiled=True)  128 us
    reduce_scatter x1, waiting for transfers between devices, per_device(): lax.psum_scatter(jnp.dot(attended, out_weight, preferred_element_type=jnp...  23.3 us
    dot_general x1, matrix products, online_update(): jnp.einsum('thgj,jhd->thgd', weights.astype(jnp.bfloat16), value_part, pr...  16.3 us
    dot_general x1, matrix products, online_update(): jnp.einsum('thgd,jhd->thgj', query_heads, key_part, preferred_element_typ...  15.7 us
    reduce_sum x1, other arithmetic, online_update(): row_total = jnp.sum(weights, axis=-1)  14.3 us
  transfers between devices with their start and end apart: 3, of which 3 were waited for; matrix products, arithmetic and copies ran while one was open for 0% of the time, Pallas kernels for 0%

commit v1 on v0

--- a/solution.py
+++ b/solution.py
@@ -6,6 +6,13 @@
 HD = 128
 GROUP = 4
 NEGATIVE = -1e30
+
+
+def swapped_in(x, name, dim):
+    count = lax.axis_size(name)
+    tiles = jnp.stack([x for _ in range(count)])
+    tiles = lax.all_to_all(tiles, name, split_axis=0, concat_axis=0)
+    return jnp.concatenate(tiles, axis=dim)
 
 
 def online_update(running, query_heads, key_part, value_part, allowed):
@@ -52,7 +59,7 @@
     sinks_here = lax.dynamic_slice_in_dim(sink_len, first_head, local_heads)
     windows_here = lax.dynamic_slice_in_dim(window_len, first_head, local_heads)
     query_heads = queries.reshape(row_count, local_heads, GROUP, HD)
-    key_part = lax.all_gather(key_states, "ctx", axis=0, tiled=True).reshape(-1, local_heads, HD)
+    key_part = swapped_in(key_states, "ctx", 0).reshape(-1, local_heads, HD)
     value_part = lax.all_gather(value_states, "ctx", axis=0, tiled=True).reshape(
         -1, local_heads, HD
     )

time: 374 us -> 275 us (0.74)
  waiting for transfers between devices: 284 us -> 167 us
  starting transfers between devices: 0.08 us -> 15.5 us
    all_gather x1 -> x0, waiting for transfers between devices: 131 us -> none  [per_device(): lax.all_gather(key_states, 'ctx', axis=0, tiled=True)]
    all_to_all x0 -> x1, waiting for transfers between devices: none -> 99.9 us  [swapped_in(): tiles = lax.all_to_all(tiles, name, split_axis=0, concat_axis=0)]
    all_gather x1, waiting for transfers between devices: 128 us -> 43.3 us  [per_device(): lax.all_gather(value_states, 'ctx', axis=0, tiled=True)]
    all_to_all x0 -> x1, starting transfers between devices: none -> 15.4 us  [swapped_in(): tiles = lax.all_to_all(tiles, name, split_axis=0, concat_axis=0)]
    another operation x0 -> x2, local copies, waits for them, and re-layouts: none -> 10.2 us  [the longest x1 6.9 us: per_device(): key_part = swapped_in(key_states, 'ctx', 0).reshape(-1, local_heads, HD)]
    reshape x1 -> x0, local copies, waits for them, and re-layouts: 6.89 us -> none  [per_device(): lax.all_gather(key_states, 'ctx', axis=0, tiled=True)]
where the time goes in v1:
time: 275 us; the launch traced here: 274 us
  waiting for transfers between devices  167 us (61%)
  matrix products  37.7 us (14%)
  other arithmetic  22.3 us (8%)
  local copies, waits for them, and re-layouts  17.7 us (6%)
  starting transfers between devices  15.5 us (6%)
  between operations  13.5 us (5%)
    all_to_all x1, waiting for transfers between devices, swapped_in(): tiles = lax.all_to_all(tiles, name, split_axis=0, concat_axis=0)  99.9 us
    all_gather x1, waiting for transfers between devices, per_device(): lax.all_gather(value_states, 'ctx', axis=0, tiled=True)  43.3 us
    reduce_scatter x1, waiting for transfers between devices, per_device(): lax.psum_scatter(jnp.dot(attended, out_weight, preferred_element_type=jnp...  23.3 us
    dot_general x1, matrix products, online_update(): jnp.einsum('thgj,jhd->thgd', weights.astype(jnp.bfloat16), value_part, pr...  16.3 us
    dot_general x1, matrix products, online_update(): jnp.einsum('thgd,jhd->thgj', query_heads, key_part, preferred_element_typ...  15.7 us
    all_to_all x1, starting transfers between devices, swapped_in(): tiles = lax.all_to_all(tiles, name, split_axis=0, concat_axis=0)  15.4 us
    reduce_sum x1, other arithmetic, online_update(): row_total = jnp.sum(weights, axis=-1)  14.3 us
    another operation x1, local copies, waits for them, and re-layouts, per_device(): key_part = swapped_in(key_states, 'ctx', 0).reshape(-1, local_heads, HD)  6.9 us
  transfers between devices with their start and end apart: 3, of which 3 were waited for; matrix products, arithmetic and copies ran while one was open for 0% of the time, Pallas kernels for 0%

profile of v1, /device:TPU:1, one launch (start us, length us, event | category | flops | bytes accessed | tf_op | source)
XLA Modules:
  0.0 273.8 jit_solution(11058487967578582545)
XLA Ops:
  6.5 3.3 %stack.2 = bf16[64,128,256]{2,1,0:T(8,128)(2,1)} broadcast(bf16[128,256]{1,0:T(8,128)(2,1)} %param.10), dimensions={1,2} | broadcast | bytes 4259840 | tf_op jit(solution)/shard_map/stack | solution.py:13
  9.9 15.4 %all-to-all-start = ((bf16[64,128,256]{2,1,0:T(8,128)(2,1)}), bf16[64,128,256]{2,1,0:T(8,128)(2,1)}, u32[]{:S(2)}, u32[]{:S(2)}) async-start(bf16[64,128,256]{2,1,0:T(8,128)(2,1)} %stack.2), calls=%async_computation | async-start | bytes 8388608 | tf_op jit(solution)/shard_map/all_to_all | solution.py:14
  25.3 0.0 all-gather.2.cloned.1.call-start
  25.3 0.7 all-gather.2.cloned.1.call-update
  26.1 99.9 %all-to-all-done = bf16[64,128,256]{2,1,0:T(8,128)(2,1)} async-done(((bf16[64,128,256]{2,1,0:T(8,128)(2,1)}), bf16[64,128,256]{2,1,0:T(8,128)(2,1)}, u32[]{:S(2)}, u32[]{:S(2)}) %all-to-all-start) | async-done | bytes 4194336 | tf_op jit(solution)/shard_map/all_to_all | solution.py:14
  125.9 43.3 %all-gather.2.cloned.1.call-done = bf16[8192,256]{1,0:T(8,128)(2,1)} async-done(((bf16[128,256]{1,0:T(8,128)(2,1)}), bf16[8192,256]{1,0:T(8,128)(2,1)}) %all-gather.2.cloned.1.call-update) | async-done | bytes 4194320 | tf_op jit(solution)/shard_map/all_gather | solution.py:63
  169.2 68.7 %conditional.1 = (f32[128,2,4]{0,2,1:T(4,128)S(1)}, f32[128,2,4,128]{0,3,2,1:T(8,128)S(1)}) conditional(s32[]{:T(128)} %convert_element_type.15, () %tuple.22, (s32[8192]{0:T(1024)S(1)}, s32[8192]{0:T(1024)S(1)}, s32[]{:T(128)}, s32[128]{0:T(128)S(1)}, s32[]{:T(128)}, /*index=5*/s32[8]{0:T(128)S(1)}, s32[8192]{0:T(1024)S(1)}, s32[8]{0:T(128)S(1)}, ...), branch_computations={%region_0.0_spmd, %region_1.4_spmd} | conditional | flops 4395662336 | bytes 147220624 | solution.py:81
  169.3 0.1 dynamic-slice_compare_fusion
  169.3 0.1 dynamic_slice.19
  169.4 0.1 compare_or_fusion
  169.5 0.1 dynamic_slice.20
  169.6 1.2 broadcast_subtract_fusion
  170.8 3.7 %broadcast_compare_fusion = pred[128,8192]{0,1:T(8,128)(4,1)S(1)} fusion(s32[128]{0:T(128)S(1)} %broadcast_add_fusion, s32[8192]{0:T(1024)S(1)} %get-tuple-element.121), kind=kLoop, calls=%fused_computation.14 | loop fusion | flops 1048576 | bytes 1081856 | tf_op jit(solution)/shard_map/cond/branch_1_fun/le | solution.py:71
  174.6 2.8 %or_and_fusion = pred[128,2,8192]{0,2,1:T(8,128)(4,1)S(1)} fusion(s32[128,8192]{0,1:T(8,128)S(1)} %broadcast_subtract_fusion, s32[2]{0:T(128)S(1)} %dynamic_slice.20, pred[2,8192]{1,0:T(4,128)(4,1)S(1)} %compare_or_fusion, pred[128,8192]{0,1:T(8,128)(4,1)S(1)} %broadcast_compare_fusion), kind=kLoop, calls=%fused_computation.9 | loop fusion | flops 6291456 | bytes 7356424 | tf_op jit(solution)/shard_map/cond/branch_1_fun/and | solution.py:71
  177.4 6.9 %reshape_reshape.6 = bf16[8192,2,128]{2,1,0:T(2,128)(2,1)} reshape(bf16[64,128,256]{2,1,0:T(8,128)(2,1)} %get-tuple-element.125) | data formatting | bytes 8388608 | tf_op jit(solution)/shard_map/reshape;reshape | solution.py:62
  184.3 0.2 reshape.121
  184.5 15.7 %fusion = (f32[128,2,4]{0,2,1:T(4,128)S(1)}, f32[2,8192,128,4]{2,1,3,0:T(8,128)}) fusion(pred[128,2,8192]{0,2,1:T(8,128)(4,1)S(1)} %or_and_fusion, bf16[128,2,4,128]{3,2,1,0:T(4,128)(2,1)S(1)} %reshape.121, bf16[8192,2,128,1]{2,1,0,3:T(2,128)(2,1)} %bitcast.23), kind=kOutput, calls=%fused_computation.2 | convolution fusion | flops 2172648448 | bytes 40112128 | tf_op jit(solution)/shard_map/cond/branch_1_fun/thgd,jhd->thgj/dot_general | solution.py:20
  200.2 6.9 %reshape.122 = bf16[8192,2,128]{2,1,0:T(2,128)(2,1)} reshape(bf16[8192,256]{1,0:T(8,128)(2,1)} %get-tuple-element.127) | data formatting | bytes 8388608 | tf_op jit(solution)/shard_map/reshape | solution.py:63
  207.1 16.3 %fusion.11 = f32[128,2,4,128]{3,0,2,1:T(8,128)S(1)} fusion(bf16[8192,2,128,1]{2,1,0,3:T(2,128)(2,1)} %bitcast.24, f32[2,8192,128,4]{2,1,3,0:T(8,128)} %get-tuple-element.142, f32[128,2,4]{0,2,1:T(4,128)S(1)} %broadcast_maximum_fusion, pred[128,2,8192]{0,2,1:T(8,128)(4,1)S(1)} %or_and_fusion), kind=kOutput, calls=%fused_computation.15 | convolution fusion | flops 2181038080 | bytes 40374272 | tf_op jit(solution)/shard_map/cond/branch_1_fun/thgj,jhd->thgd/dot_general | solution.py:28
  223.4 0.2 copy.36
  223.6 14.3 %fusion.4 = f32[128,2,4]{0,2,1:T(4,128)S(1)} fusion(f32[2,8192,128,4]{2,1,3,0:T(8,128)} %get-tuple-element.142, f32[128,2,4]{0,2,1:T(4,128)S(1)} %broadcast_maximum_fusion, pred[128,2,8192]{0,2,1:T(8,128)(4,1)S(1)} %or_and_fusion), kind=kLoop, calls=%fused_computation.6 | loop fusion | flops 33553408 | bytes 35659776 | tf_op jit(solution)/shard_map/cond/branch_1_fun/reduce_sum | solution.py:27
  237.9 0.1 divide_convert_fusion
  238.0 5.6 %convolution_convert_fusion = bf16[128,4096]{1,0:T(8,128)(2,1)} fusion(bf16[128,1024]{0,1:T(8,128)(2,1)S(1)} %bitcast.25, bf16[1024,4096]{1,0:T(8,128)(2,1)} %param.12), kind=kOutput, calls=%fused_computation.23 | convolution fusion | flops 1074266112 | bytes 9699328 | tf_op jit(solution)/shard_map/dot_general | solution.py:86
  243.7 23.3 %reduce-scatter.2.cloned.1.call-done = bf16[32,4096]{1,0:T(8,128)(2,1)} async-done(((bf16[128,4096]{1,0:T(8,128)(2,1)}), bf16[32,4096]{1,0:T(8,128)(2,1)}) %reduce-scatter.2.cloned.1.call-update) | async-done | bytes 262160 | tf_op jit(solution)/shard_map/reduce_scatter | solution.py:85
  (14 shorter events, 0.1 us)
Async XLA Ops:
  6.5 162.7 %copy-start.1 = (s32[8]{0:T(128)S(1)}, s32[8]{0:T(128)}, u32[]{:S(2)}) copy-start(s32[8]{0:T(128)} %param.13) | copy-start | bytes 100
  6.5 162.7 %copy-start.2 = (s32[8]{0:T(128)S(1)}, s32[8]{0:T(128)}, u32[]{:S(2)}) copy-start(s32[8]{0:T(128)} %param.14) | copy-start | bytes 100
  6.5 162.7 %copy-start.3 = (s32[8]{0:T(128)S(1)}, s32[8]{0:T(128)}, u32[]{:S(2)}) copy-start(s32[8]{0:T(128)} %param.15) | copy-start | bytes 100
  6.5 162.7 %copy-start = (bf16[128,1024]{1,0:T(8,128)(2,1)S(1)}, bf16[128,1024]{1,0:T(8,128)(2,1)}, u32[]{:S(2)}) copy-start(bf16[128,1024]{1,0:T(8,128)(2,1)} %param.9) | copy-start | bytes 786436
  9.9 116.0 %all-to-all-start = ((bf16[64,128,256]{2,1,0:T(8,128)(2,1)}), bf16[64,128,256]{2,1,0:T(8,128)(2,1)}, u32[]{:S(2)}, u32[]{:S(2)}) async-start(bf16[64,128,256]{2,1,0:T(8,128)(2,1)} %stack.2), calls=%async_computation | async-start | bytes 8388608 | tf_op jit(solution)/shard_map/all_to_all | solution.py:14
  25.3 143.9 %all-gather.2.cloned.1.call-start = ((), (), s32[]{:S(2)}) async-start(), calls=%async_computation.2 | async-start | bytes 4259840 | tf_op jit(solution)/shard_map/all_gather | solution.py:63
  26.0 241.0 %reduce-scatter.2.cloned.1.call-start = ((), (), s32[]{:S(2)}) async-start(), calls=%async_computation.3 | async-start | bytes 1310720 | tf_op jit(solution)/shard_map/reduce_scatter | solution.py:85
Sparse Core Ops, SparseCore 0:
  29.6 139.5 all-gather.1
  243.8 23.1 reduce-scatter.1
